TPU v7x, 128 devices: a whole 4x4x4 slice. The times are simulated.
128 devices in a mesh: expert: 32 (over y, x_hi, z), tensor: 4 (over x_lo, core).
Axes of the slice: x: 4 (x_hi: 2, x_lo: 2; x = x_hi * 2 + x_lo), y: 4, z: 4, core: 2. Of those that a mesh axis runs over, the one named last changes fastest.
Arguments:
- hidden_in: bfloat16 [16384, 4096], P(('expert', 'tensor')), may hold values from -20 to 20
- context: bfloat16 [16384, 4096], P('expert', 'tensor'), may hold values from -6 to 6
- w_out: bfloat16 [4096, 4096], P('tensor', 'expert'), may hold values from -0.09375 to 0.09375
- norm_gain: float32 [4096], replicated, may hold values from 0.25 to 1.75
- expert_ids: int32 [16384, 8], P(('expert', 'tensor')), may hold values from 0 to 127, all different within a row; in each aligned block of 128 rows (0 to 127, 128 to 255, ...) at most 9 rows name the same one
- route_weight: float32 [16384, 8], P(('expert', 'tensor')), may hold values from 0.05 to 1
- w_gate_up: bfloat16 [128, 4096, 1536], P(('expert', 'tensor')), may hold values from -0.09375 to 0.09375
- w_down: bfloat16 [128, 768, 4096], P(('expert', 'tensor')), may hold values from -0.21875 to 0.21875
Outputs:
- attended: bfloat16 [16384, 4096], P(('expert', 'tensor'))
- mixed: bfloat16 [16384, 4096], P(('expert', 'tensor'))
Inputs may be any that keep to these rules, and one draw needn't show every extreme that they name: `expert_ids`: each row names 8 different experts. Among the 128 rows of one device no expert is named more than 9 times, and in every draw some expert is named exactly 9 times by the rows of some device.
All inputs are finite; a program needn't handle non-finite values.
Results may differ from a plain program's by a relative error of at most 0.0053.
Values may be sent and summed in bfloat16 or wider, within the bound.
A program may use at most 128 MiB of HBM per device.

v0:
```python
import jax
import jax.numpy as jnp
import numpy as np
from jax import lax
from jax.sharding import Mesh
from jax.sharding import PartitionSpec as P

LANES = 128
ALL = ("expert", "xlo", "core")


def expert_block(received, w_gate_up, w_down):
    hidden_units = w_down.shape[1]
    gate_and_up = jnp.dot(received, w_gate_up[0], preferred_element_type=jnp.float32)
    activated = (jax.nn.silu(gate_and_up[:, :hidden_units]) * gate_and_up[:, hidden_units:]).astype(
        jnp.bfloat16
    )
    return jnp.dot(activated, w_down[0], preferred_element_type=jnp.float32).astype(jnp.bfloat16)


def project(context, w_out):
    n_x = lax.axis_size("xlo")
    n_c = lax.axis_size("core")
    rows = context.shape[0] // (n_x * n_c)
    context = (
        context.reshape(n_x, n_c, rows, -1).transpose(1, 0, 2, 3).reshape(n_x * n_c * rows, -1)
    )
    partial_sums = jnp.dot(
        context,
        lax.all_gather(w_out, "expert", axis=1, tiled=True),
        preferred_element_type=jnp.float32,
    )
    width = partial_sums.shape[1]
    chip_sums = lax.psum_scatter(partial_sums, "core", scatter_dimension=0, tiled=True)
    chip_sums = chip_sums.reshape(n_x, rows, width)
    me = lax.axis_index("xlo")
    own = lax.dynamic_index_in_dim(chip_sums, me, axis=0, keepdims=False)
    other = lax.dynamic_index_in_dim(chip_sums, 1 - me, axis=0, keepdims=False)
    arrived = lax.ppermute(other.astype(jnp.bfloat16), "xlo", perm=[(0, 1), (1, 0)])
    return own + arrived.astype(jnp.float32)


def on_device(hidden_in, context, w_out, norm_gain, expert_ids, route_weight, w_gate_up, w_down):
    tok_count, width = hidden_in.shape
    chunks = width // LANES
    projected = project(context, w_out)
    residual = hidden_in.astype(jnp.float32) + projected
    attended = residual.astype(jnp.bfloat16)
    inverse = lax.rsqrt(jnp.mean(residual * residual, axis=1, keepdims=True) + 1e-06)
    normed = (residual * inverse * norm_gain[None, :]).astype(jnp.bfloat16)
    top_count = expert_ids.shape[1]
    experts_all = lax.axis_size(ALL)
    capacity = tok_count * top_count * 9 // (8 * experts_all)
    rows_all = experts_all * capacity
    chosen = expert_ids.reshape(-1)
    onehot = (chosen[:, None] == jnp.arange(experts_all, dtype=jnp.int32)[None, :]).astype(
        jnp.int32
    )
    before = jnp.cumsum(onehot, axis=0) - onehot
    slots = jnp.sum(before * onehot, axis=1)
    target = chosen * capacity + slots
    token_index = jnp.arange(tok_count * top_count, dtype=jnp.int32) // top_count
    source = jnp.full((rows_all,), tok_count, jnp.int32).at[target].set(token_index)
    normed3 = jnp.concatenate(
        [normed.reshape(tok_count, chunks, LANES), jnp.zeros((1, chunks, LANES), jnp.bfloat16)],
        axis=0,
    )
    send = jnp.take(normed3, source, axis=0)
    send = send.reshape(experts_all, capacity * chunks, LANES)
    received = lax.all_to_all(send, ALL, split_axis=0, concat_axis=0, tiled=True)
    outputs = expert_block(received.reshape(rows_all, width), w_gate_up, w_down)
    outputs = outputs.reshape(experts_all, capacity * chunks, LANES)
    returned = lax.all_to_all(outputs, ALL, split_axis=0, concat_axis=0, tiled=True)
    returned = returned.reshape(rows_all, chunks, LANES)
    picked = jnp.take(returned, target, axis=0).reshape(tok_count, top_count, chunks, LANES)
    moe_sum = jnp.sum(route_weight[:, :, None, None] * picked.astype(jnp.float32), axis=1)
    mixed = (residual + moe_sum.reshape(tok_count, width)).astype(jnp.bfloat16)
    return (attended, mixed)


def solution(mesh):
    n_expert = mesh.shape["expert"]
    n_tensor = mesh.shape["tensor"]
    n_core = 2 if n_tensor % 2 == 0 else 1
    devices = np.asarray(mesh.devices).reshape(n_expert, n_tensor // n_core, n_core)
    mesh3 = Mesh(devices, ALL)
    tensor = ("xlo", "core")
    in_specs = (
        P(ALL, None),
        P("expert", tensor),
        P(tensor, "expert"),
        P(),
        P(ALL, None),
        P(ALL, None),
        P(ALL, None, None),
        P(ALL, None, None),
    )
    out_specs = (P(ALL, None), P(ALL, None))
    return jax.shard_map(
        on_device, mesh=mesh3, in_specs=in_specs, out_specs=out_specs, check_vma=False
    )
```

profile of v0, /device:TPU:54, one launch (start us, length us, event | category | flops | bytes accessed | tf_op | source)
XLA Modules:
  0.0 561.1 jit_solution(10142530440497520180)
XLA Ops:
  7.2 0.0 all-gather.2.cloned.1.call-start
  7.2 0.7 all-gather.2.cloned.1.call-update
  7.9 0.0 reduce-scatter.2.cloned.1.call-start
  7.9 1.3 copy.29
  9.2 131.0 %all-gather.2.cloned.1.call-done = bf16[1024,4096]{1,0:T(8,128)(2,1)} async-done(((bf16[1024,128]{1,0:T(8,128)(2,1)}), bf16[1024,4096]{1,0:T(8,128)(2,1)}) %all-gather.2.cloned.1.call-update) | async-done | bytes 8388624 | tf_op jit(solution)/shard_map/all_gather | solution.py:30
  140.2 10.0 %fusion.22 = f32[512,4096]{1,0:T(8,128)} fusion(bf16[512,1024]{1,0:T(8,128)(2,1)S(1)} %bitcast.54, bf16[1024,4096]{1,0:T(8,128)(2,1)} %all-gather.2.cloned.1.call-done), kind=kOutput, calls=%fused_computation.50 | convolution fusion | flops 4294967296 | bytes 17825792 | tf_op jit(solution)/shard_map/dot_general | solution.py:28
  150.3 0.0 copy-start
  150.3 0.0 reduce-scatter.2.cloned.1.call-update
  150.3 0.0 copy-start.1
  150.3 0.6 copy-done
  151.0 0.1 copy.31
  151.1 0.1 eq.26
  151.2 0.1 copy.33
  151.3 0.2 fusion.12
  151.6 19.2 %reduce-scatter.2.cloned.1.call-done = f32[256,4096]{1,0:T(8,128)} async-done(((f32[512,4096]{1,0:T(8,128)}), f32[256,4096]{1,0:T(8,128)}) %reduce-scatter.2.cloned.1.call-update) | async-done | bytes 4194320 | tf_op jit(solution)/shard_map/reduce_scatter | solution.py:34
  170.8 1.7 fusion.8
  172.5 0.9 collective-permute-start
  173.5 0.1 reshape.112
  173.5 0.1 copy.34
  173.7 0.1 copy.37
  173.8 0.1 mul.60
  173.9 0.4 fusion.11
  174.2 4.3 scatter_custom_fusion
  178.6 0.2 broadcast_in_dim.39
  178.8 0.1 copy.38
  178.9 0.2 copy.39
  179.1 18.9 %collective-permute-done = bf16[128,4096]{1,0:T(8,128)(2,1)} collective-permute-done((bf16[128,4096]{1,0:T(8,128)(2,1)S(1)}, bf16[128,4096]{1,0:T(8,128)(2,1)}, u32[]{:S(2)}, u32[]{:S(2)}) %collective-permute-start) | collective-permute-done | bytes 1048608 | tf_op jit(solution)/shard_map/ppermute | solution.py:39
  198.0 2.7 multiply_reduce_fusion.1
  200.7 0.0 copy-done.1
  200.7 0.3 fusion.9
  201.1 0.2 copy.40
  201.3 0.2 concatenate.3
  201.5 6.1 %gather_fusion = bf16[1152,32,128]{2,1,0:T(8,128)(2,1)} fusion(bf16[129,32,128]{2,1,0:T(8,128)(2,1)S(1)} %concatenate.3, s32[2048]{0:T(1024)S(1)} %pad_clamp_fusion), kind=kCustom, calls=%fused_computation | custom fusion | bytes 18878976 | tf_op jit(solution)/shard_map/jit(_take)/gather | solution.py:68
  207.6 8.9 %bitcast_select_fusion = bf16[128,288,128]{2,1,0:T(8,128)(2,1)S(1)} fusion(pred[128,288]{1,0:T(8,128)(4,1)S(1)} %copy.39, bf16[128,288,128]{2,1,0:T(8,128)(2,1)} %bitcast.48), kind=kLoop, calls=%fused_computation.7 | loop fusion | flops 4718592 | bytes 18911232 | tf_op jit(solution)/shard_map/jit(_take)/select_n | solution.py:68
  216.5 120.5 %all_to_all.10 = bf16[128,288,128]{2,1,0:T(8,128)(2,1)} all-to-all(bf16[128,288,128]{2,1,0:T(8,128)(2,1)S(1)} %bitcast_select_fusion), channel_id=1, replica_groups=mesh['expert'=32,'xlo'=2,'core'=2] {'expert','xlo','core'}, dimensions={0} | all-to-all | bytes 18874368 | tf_op jit(solution)/shard_map/all_to_all | solution.py:70
  337.0 14.8 %reshape.115 = bf16[1152,4096]{1,0:T(8,128)(2,1)} reshape(bf16[128,288,128]{2,1,0:T(8,128)(2,1)} %all_to_all.10) | data formatting | bytes 18874368 | tf_op jit(solution)/shard_map/reshape | solution.py:71
  351.8 18.2 %fusion = f32[1152,1536]{1,0:T(8,128)S(1)} fusion(bf16[1152,4096]{1,0:T(8,128)(2,1)} %reshape.115, bf16[1,4096,1536]{2,1,0:T(8,128)(2,1)} %param.14), kind=kOutput, calls=%fused_computation.5 | convolution fusion | flops 14495514624 | bytes 29097984 | tf_op jit(solution)/shard_map/dot_general | solution.py:14
  370.1 12.5 %convolution_convert_fusion = bf16[1152,4096]{1,0:T(8,128)(2,1)} fusion(bf16[1,768,4096]{2,1,0:T(8,128)(2,1)} %param.15, f32[1152,1536]{1,0:T(8,128)S(1)} %fusion), kind=kOutput, calls=%fused_computation.4 | convolution fusion | flops 7257784320 | bytes 22806528 | tf_op jit(solution)/shard_map/dot_general | solution.py:18
  382.6 15.0 %reshape.116 = bf16[128,288,128]{2,1,0:T(8,128)(2,1)} reshape(bf16[1152,4096]{1,0:T(8,128)(2,1)} %convolution_convert_fusion) | data formatting | bytes 18874368 | tf_op jit(solution)/shard_map/reshape | solution.py:72
  397.6 0.0 copy-start.2
  397.6 10.0 %all-to-all-start.1 = ((bf16[128,288,128]{2,1,0:T(8,128)(2,1)}), bf16[128,288,128]{2,1,0:T(8,128)(2,1)}, u32[]{:S(2)}, u32[]{:S(2)}) async-start(bf16[128,288,128]{2,1,0:T(8,128)(2,1)} %reshape.116), calls=%async_computation.2 | async-start | bytes 18874368 | tf_op jit(solution)/shard_map/all_to_all | solution.py:73
  407.6 0.1 reduce_sum.32
  407.7 0.1 copy.36
  407.9 0.0 copy-done.2
  407.9 0.1 copy.30
  408.0 121.9 %all-to-all-done.1 = bf16[128,288,128]{2,1,0:T(8,128)(2,1)} async-done(((bf16[128,288,128]{2,1,0:T(8,128)(2,1)}), bf16[128,288,128]{2,1,0:T(8,128)(2,1)}, u32[]{:S(2)}, u32[]{:S(2)}) %all-to-all-start.1) | async-done | bytes 9437216 | tf_op jit(solution)/shard_map/all_to_all | solution.py:73
  529.9 13.5 %gather_fusion.1 = bf16[1024,32,128]{2,1,0:T(8,128)(2,1)} fusion(bf16[1152,32,128]{2,1,0:T(8,128)(2,1)} %bitcast.15, s32[1024]{0:T(1024)S(1)} %broadcast_clamp_fusion), kind=kCustom, calls=%fused_computation.1 | custom fusion | bytes 16781312 | tf_op jit(solution)/shard_map/jit(_take)/gather | solution.py:75
  543.4 8.2 %multiply_reduce_fusion = f32[128,32,128]{2,1,0:T(8,128)S(1)} fusion(f32[128,8]{1,0:T(8,128)S(1)} %copy.30, pred[128,8]{1,0:T(8,128)(4,1)S(1)} %copy.36, bf16[1024,32,128]{2,1,0:T(8,128)(2,1)} %gather_fusion.1), kind=kLoop, calls=%fused_computation.3 | loop fusion | flops 16252928 | bytes 10490880 | tf_op jit(solution)/shard_map/reduce_sum | solution.py:76
  551.6 2.6 fusion.4
  (15 shorter events, 0.2 us)
Async XLA Ops:
  7.2 133.1 %all-gather.2.cloned.1.call-start = ((), (), s32[]{:S(2)}) async-start(), calls=%async_computation.3 | async-start | bytes 8650752 | tf_op jit(solution)/shard_map/all_gather | solution.py:30
  7.9 162.9 %reduce-scatter.2.cloned.1.call-start = ((), (), s32[]{:S(2)}) async-start(), calls=%async_computation.4 | async-start | bytes 12582912 | tf_op jit(solution)/shard_map/reduce_scatter | solution.py:34
  150.3 0.7 copy-start
  150.3 50.4 %copy-start.1 = (f32[4096]{0:T(1024)S(1)}, f32[4096]{0:T(1024)}, u32[]{:S(2)}) copy-start(f32[4096]{0:T(1024)} %param.11) | copy-start | bytes 49156
  172.5 25.5 %collective-permute-start = (bf16[128,4096]{1,0:T(8,128)(2,1)S(1)}, bf16[128,4096]{1,0:T(8,128)(2,1)}, u32[]{:S(2)}, u32[]{:S(2)}) collective-permute-start(bf16[128,4096]{1,0:T(8,128)(2,1)S(1)} %fusion.8), channel_id=1, source_target_pairs={{0,2},{2,0},{1,3},{3,1},{4,6},{6,4},{5,7},{7,5},{8,10},{10,8},{9,1... | collective-permute-start | bytes 3145736 | tf_op jit(solution)/shard_map/ppermute | solution.py:39
  397.6 10.3 %copy-start.2 = (f32[128,8]{0,1:T(8,128)S(1)}, f32[128,8]{0,1:T(8,128)}, u32[]{:S(2)}) copy-start(f32[128,8]{0,1:T(8,128)} %param.13) | copy-start | bytes 12292
  397.6 132.3 %all-to-all-start.1 = ((bf16[128,288,128]{2,1,0:T(8,128)(2,1)}), bf16[128,288,128]{2,1,0:T(8,128)(2,1)}, u32[]{:S(2)}, u32[]{:S(2)}) async-start(bf16[128,288,128]{2,1,0:T(8,128)(2,1)} %reshape.116), calls=%async_computation.2 | async-start | bytes 18874368 | tf_op jit(solution)/shard_map/all_to_all | solution.py:73
Sparse Core Ops, SparseCore 0:
  10.7 129.4 all-gather.1
  150.4 20.3 reduce-scatter.1
where the time goes:
time: 562 us; the launch traced here: 561 us
  waiting for transfers between devices  292 us (52%)
  blocking collectives  120 us (21%)
  local copies, waits for them, and re-layouts  59.4 us (11%)
  matrix products  40.8 us (7%)
  other arithmetic  23.4 us (4%)
  between operations  14.3 us (3%)
  starting transfers between devices  11 us (2%)
    all_gather x1, waiting for transfers between devices, project(): lax.all_gather(w_out, 'expert', axis=1, tiled=True)  131 us
    all_to_all x1, waiting for transfers between devices, on_device(): lax.all_to_all(outputs, ALL, split_axis=0, concat_axis=0, tiled=True)  122 us
    all_to_all x1, blocking collectives, on_device(): lax.all_to_all(send, ALL, split_axis=0, concat_axis=0, tiled=True)  120 us
    reduce_scatter x1, waiting for transfers between devices, project(): lax.psum_scatter(partial_sums, 'core', scatter_dimension=0, tiled=True)  19.2 us
    ppermute x1, waiting for transfers between devices, project(): lax.ppermute(other.astype(jnp.bfloat16), 'xlo', perm=[(0, 1), (1, 0)])  18.9 us
    dot_general x1, matrix products, expert_block(): jnp.dot(received, w_gate_up[0], preferred_element_type=jnp.float32)  18.2 us
    reshape x1, local copies, waits for them, and re-layouts, on_device(): outputs = outputs.reshape(experts_all, capacity * chunks, LANES)  15 us
    reshape x1, local copies, waits for them, and re-layouts, on_device(): outputs = expert_block(received.reshape(rows_all, width), w_gate_up, w_down)  14.8 us
  transfers between devices with their start and end apart: 4, of which 4 were waited for; matrix products, arithmetic and copies ran while one was open for 1% of the time, Pallas kernels for 0%

commit v1 on v0

--- a/solution.py
+++ b/solution.py
@@ -7,6 +7,12 @@
 
 LANES = 128
 ALL = ("expert", "xlo", "core")
+
+
+def _step_on_quarters(point, device_axis):
+    return jnp.concatenate(
+        lax.all_to_all(jnp.stack([point] * lax.axis_size(device_axis)), device_axis, 0, 0), axis=1
+    )
 
 
 def expert_block(received, w_gate_up, w_down):
@@ -26,9 +32,7 @@
         context.reshape(n_x, n_c, rows, -1).transpose(1, 0, 2, 3).reshape(n_x * n_c * rows, -1)
     )
     partial_sums = jnp.dot(
-        context,
-        lax.all_gather(w_out, "expert", axis=1, tiled=True),
-        preferred_element_type=jnp.float32,
+        context, _step_on_quarters(w_out, "expert"), preferred_element_type=jnp.float32
     )
     width = partial_sums.shape[1]
     chip_sums = lax.psum_scatter(partial_sums, "core", scatter_dimension=0, tiled=True)

time: 562 us -> 583 us (1.037)
  starting transfers between devices: 11 us -> 21.5 us
    all_gather x1 -> x0, waiting for transfers between devices: 131 us -> none  [project(): lax.all_gather(w_out, 'expert', axis=1, tiled=True)]
    all_to_all x0 -> x1, waiting for transfers between devices: none -> 123 us  [_step_on_quarters(): lax.all_to_all(jnp.stack([point] * lax.axis_size(device_axis)), device_ax...]
    reduce_scatter x1, waiting for transfers between devices: 19.2 us -> 33.1 us  [project(): lax.psum_scatter(partial_sums, 'core', scatter_dimension=0, tiled=True)]
    all_to_all x0 -> x1, starting transfers between devices: none -> 10.6 us  [_step_on_quarters(): lax.all_to_all(jnp.stack([point] * lax.axis_size(device_axis)), device_ax...]
where the time goes in v1:
time: 583 us; the launch traced here: 581 us
  waiting for transfers between devices  297 us (51%)
  blocking collectives  121 us (21%)
  local copies, waits for them, and re-layouts  63.6 us (11%)
  matrix products  40.8 us (7%)
  other arithmetic  23.4 us (4%)
  starting transfers between devices  21.5 us (4%)
  between operations  14.3 us (2%)
    all_to_all x1, waiting for transfers between devices, _step_on_quarters(): lax.all_to_all(jnp.stack([point] * lax.axis_size(device_axis)), device_ax...  123 us
    all_to_all x1, waiting for transfers between devices, on_device(): lax.all_to_all(outputs, ALL, split_axis=0, concat_axis=0, tiled=True)  122 us
    all_to_all x1, blocking collectives, on_device(): lax.all_to_all(send, ALL, split_axis=0, concat_axis=0, tiled=True)  121 us
    reduce_scatter x1, waiting for transfers between devices, project(): lax.psum_scatter(partial_sums, 'core', scatter_dimension=0, tiled=True)  33.1 us
    ppermute x1, waiting for transfers between devices, project(): lax.ppermute(other.astype(jnp.bfloat16), 'xlo', perm=[(0, 1), (1, 0)])  18.8 us
    dot_general x1, matrix products, expert_block(): jnp.dot(received, w_gate_up[0], preferred_element_type=jnp.float32)  18.2 us
    reshape x1, local copies, waits for them, and re-layouts, on_device(): outputs = outputs.reshape(experts_all, capacity * chunks, LANES)  15 us
    reshape x1, local copies, waits for them, and re-layouts, on_device(): outputs = expert_block(received.reshape(rows_all, width), w_gate_up, w_down)  14.8 us
  transfers between devices with their start and end apart: 4, of which 4 were waited for; matrix products, arithmetic and copies ran while one was open for 1% of the time, Pallas kernels for 0%

profile of v1, /device:TPU:54, one launch (start us, length us, event | category | flops | bytes accessed | tf_op | source)
XLA Modules:
  0.0 581.5 jit_solution(17636422822209441736)
XLA Ops:
  7.2 1.1 copy.32
  8.3 4.3 stack.2
  12.5 0.0 copy-start
  12.5 10.6 %all-to-all-start = ((bf16[32,1024,128]{1,2,0:T(8,128)(2,1)}), bf16[32,1024,128]{1,2,0:T(8,128)(2,1)}, u32[]{:S(2)}, u32[]{:S(2)}) async-start(bf16[32,1024,128]{1,2,0:T(8,128)(2,1)} %stack.2), calls=%async_computation | async-start | bytes 16777216 | tf_op jit(solution)/shard_map/all_to_all | solution.py:14
  23.1 0.0 reduce-scatter.2.cloned.1.call-start
  23.2 0.0 copy-done
  23.2 0.1 copy.31
  23.3 123.5 %all-to-all-done = bf16[32,1024,128]{1,2,0:T(8,128)(2,1)} async-done(((bf16[32,1024,128]{1,2,0:T(8,128)(2,1)}), bf16[32,1024,128]{1,2,0:T(8,128)(2,1)}, u32[]{:S(2)}, u32[]{:S(2)}) %all-to-all-start) | async-done | bytes 8388640 | tf_op jit(solution)/shard_map/all_to_all | solution.py:14
  146.8 10.1 %fusion.22 = f32[512,4096]{1,0:T(8,128)} fusion(bf16[512,1024]{1,0:T(8,128)(2,1)S(1)} %bitcast.57, bf16[1024,4096]{0,1:T(8,128)(2,1)} %bitcast.4), kind=kOutput, calls=%fused_computation.50 | convolution fusion | flops 4294967296 | bytes 17825792 | tf_op jit(solution)/shard_map/dot_general | solution.py:34
  156.9 0.0 copy-start.1
  156.9 0.0 reduce-scatter.2.cloned.1.call-update
  156.9 0.0 copy-start.2
  156.9 0.6 copy-done.1
  157.6 0.1 copy.34
  157.7 0.1 eq.26
  157.7 0.1 copy.36
  157.9 0.2 fusion.12
  158.1 33.1 %reduce-scatter.2.cloned.1.call-done = f32[256,4096]{1,0:T(8,128)} async-done(((f32[512,4096]{1,0:T(8,128)}), f32[256,4096]{1,0:T(8,128)}) %reduce-scatter.2.cloned.1.call-update) | async-done | bytes 4194320 | tf_op jit(solution)/shard_map/reduce_scatter | solution.py:38
  191.2 1.7 fusion.8
  192.9 0.9 collective-permute-start
  193.9 0.1 reshape.122
  194.0 0.1 copy.37
  194.1 0.1 copy.40
  194.2 0.1 mul.60
  194.3 0.4 fusion.11
  194.7 4.3 scatter_custom_fusion
  199.0 0.2 broadcast_in_dim.39
  199.3 0.1 copy.41
  199.4 0.2 copy.42
  199.6 18.8 %collective-permute-done = bf16[128,4096]{1,0:T(8,128)(2,1)} collective-permute-done((bf16[128,4096]{1,0:T(8,128)(2,1)S(1)}, bf16[128,4096]{1,0:T(8,128)(2,1)}, u32[]{:S(2)}, u32[]{:S(2)}) %collective-permute-start) | collective-permute-done | bytes 1048608 | tf_op jit(solution)/shard_map/ppermute | solution.py:43
  218.4 2.7 multiply_reduce_fusion.1
  221.1 0.0 copy-done.2
  221.1 0.3 fusion.9
  221.5 0.2 copy.43
  221.7 0.2 concatenate.3
  221.9 6.1 %gather_fusion = bf16[1152,32,128]{2,1,0:T(8,128)(2,1)} fusion(bf16[129,32,128]{2,1,0:T(8,128)(2,1)S(1)} %concatenate.3, s32[2048]{0:T(1024)S(1)} %pad_clamp_fusion), kind=kCustom, calls=%fused_computation | custom fusion | bytes 18878976 | tf_op jit(solution)/shard_map/jit(_take)/gather | solution.py:72
  228.0 8.9 %bitcast_select_fusion = bf16[128,288,128]{2,1,0:T(8,128)(2,1)S(1)} fusion(pred[128,288]{1,0:T(8,128)(4,1)S(1)} %copy.42, bf16[128,288,128]{2,1,0:T(8,128)(2,1)} %bitcast.51), kind=kLoop, calls=%fused_computation.7 | loop fusion | flops 4718592 | bytes 18911232 | tf_op jit(solution)/shard_map/jit(_take)/select_n | solution.py:72
  236.9 120.5 %all_to_all.15 = bf16[128,288,128]{2,1,0:T(8,128)(2,1)} all-to-all(bf16[128,288,128]{2,1,0:T(8,128)(2,1)S(1)} %bitcast_select_fusion), channel_id=1, replica_groups=mesh['expert'=32,'xlo'=2,'core'=2] {'expert','xlo','core'}, dimensions={0} | all-to-all | bytes 18874368 | tf_op jit(solution)/shard_map/all_to_all | solution.py:74
  357.4 14.8 %reshape.125 = bf16[1152,4096]{1,0:T(8,128)(2,1)} reshape(bf16[128,288,128]{2,1,0:T(8,128)(2,1)} %all_to_all.15) | data formatting | bytes 18874368 | tf_op jit(solution)/shard_map/reshape | solution.py:75
  372.3 18.2 %fusion = f32[1152,1536]{1,0:T(8,128)S(1)} fusion(bf16[1152,4096]{1,0:T(8,128)(2,1)} %reshape.125, bf16[1,4096,1536]{2,1,0:T(8,128)(2,1)} %param.14), kind=kOutput, calls=%fused_computation.5 | convolution fusion | flops 14495514624 | bytes 29097984 | tf_op jit(solution)/shard_map/dot_general | solution.py:20
  390.5 12.5 %convolution_convert_fusion = bf16[1152,4096]{1,0:T(8,128)(2,1)} fusion(bf16[1,768,4096]{2,1,0:T(8,128)(2,1)} %param.15, f32[1152,1536]{1,0:T(8,128)S(1)} %fusion), kind=kOutput, calls=%fused_computation.4 | convolution fusion | flops 7257784320 | bytes 22806528 | tf_op jit(solution)/shard_map/dot_general | solution.py:24
  403.0 15.0 %reshape.126 = bf16[128,288,128]{2,1,0:T(8,128)(2,1)} reshape(bf16[1152,4096]{1,0:T(8,128)(2,1)} %convolution_convert_fusion) | data formatting | bytes 18874368 | tf_op jit(solution)/shard_map/reshape | solution.py:76
  418.0 0.0 copy-start.3
  418.0 10.0 %all-to-all-start.2 = ((bf16[128,288,128]{2,1,0:T(8,128)(2,1)}), bf16[128,288,128]{2,1,0:T(8,128)(2,1)}, u32[]{:S(2)}, u32[]{:S(2)}) async-start(bf16[128,288,128]{2,1,0:T(8,128)(2,1)} %reshape.126), calls=%async_computation.3 | async-start | bytes 18874368 | tf_op jit(solution)/shard_map/all_to_all | solution.py:77
  428.0 0.1 reduce_sum.32
  428.1 0.1 copy.39
  428.3 0.0 copy-done.3
  428.3 0.1 copy.33
  428.4 121.9 %all-to-all-done.2 = bf16[128,288,128]{2,1,0:T(8,128)(2,1)} async-done(((bf16[128,288,128]{2,1,0:T(8,128)(2,1)}), bf16[128,288,128]{2,1,0:T(8,128)(2,1)}, u32[]{:S(2)}, u32[]{:S(2)}) %all-to-all-start.2) | async-done | bytes 9437216 | tf_op jit(solution)/shard_map/all_to_all | solution.py:77
  550.3 13.5 %gather_fusion.1 = bf16[1024,32,128]{2,1,0:T(8,128)(2,1)} fusion(bf16[1152,32,128]{2,1,0:T(8,128)(2,1)} %bitcast.17, s32[1024]{0:T(1024)S(1)} %broadcast_clamp_fusion), kind=kCustom, calls=%fused_computation.1 | custom fusion | bytes 16781312 | tf_op jit(solution)/shard_map/jit(_take)/gather | solution.py:79
  563.8 8.2 %multiply_reduce_fusion = f32[128,32,128]{2,1,0:T(8,128)S(1)} fusion(f32[128,8]{1,0:T(8,128)S(1)} %copy.33, pred[128,8]{1,0:T(8,128)(4,1)S(1)} %copy.39, bf16[1024,32,128]{2,1,0:T(8,128)(2,1)} %gather_fusion.1), kind=kLoop, calls=%fused_computation.3 | loop fusion | flops 16252928 | bytes 10490880 | tf_op jit(solution)/shard_map/reduce_sum | solution.py:80
  572.0 2.6 fusion.4
  (15 shorter events, 0.2 us)
Async XLA Ops:
  12.5 10.7 %copy-start = (bf16[512,1024]{1,0:T(8,128)(2,1)S(1)}, bf16[512,1024]{1,0:T(8,128)(2,1)}, u32[]{:S(2)}) copy-start(bf16[512,1024]{1,0:T(8,128)(2,1)} %param.9) | copy-start | bytes 3145732
  12.5 134.2 %all-to-all-start = ((bf16[32,1024,128]{1,2,0:T(8,128)(2,1)}), bf16[32,1024,128]{1,2,0:T(8,128)(2,1)}, u32[]{:S(2)}, u32[]{:S(2)}) async-start(bf16[32,1024,128]{1,2,0:T(8,128)(2,1)} %stack.2), calls=%async_computation | async-start | bytes 16777216 | tf_op jit(solution)/shard_map/all_to_all | solution.py:14
  23.1 168.1 %reduce-scatter.2.cloned.1.call-start = ((), (), s32[]{:S(2)}) async-start(), calls=%async_computation.4 | async-start | bytes 12582912 | tf_op jit(solution)/shard_map/reduce_scatter | solution.py:38
  156.9 0.7 copy-start.1
  156.9 64.2 %copy-start.2 = (f32[4096]{0:T(1024)S(1)}, f32[4096]{0:T(1024)}, u32[]{:S(2)}) copy-start(f32[4096]{0:T(1024)} %param.11) | copy-start | bytes 49156
  192.9 25.5 %collective-permute-start = (bf16[128,4096]{1,0:T(8,128)(2,1)S(1)}, bf16[128,4096]{1,0:T(8,128)(2,1)}, u32[]{:S(2)}, u32[]{:S(2)}) collective-permute-start(bf16[128,4096]{1,0:T(8,128)(2,1)S(1)} %fusion.8), channel_id=1, source_target_pairs={{0,2},{2,0},{1,3},{3,1},{4,6},{6,4},{5,7},{7,5},{8,10},{10,8},{9,1... | collective-permute-start | bytes 3145736 | tf_op jit(solution)/shard_map/ppermute | solution.py:43
  418.0 10.3 %copy-start.3 = (f32[128,8]{0,1:T(8,128)S(1)}, f32[128,8]{0,1:T(8,128)}, u32[]{:S(2)}) copy-start(f32[128,8]{0,1:T(8,128)} %param.13) | copy-start | bytes 12292
  418.0 132.3 %all-to-all-start.2 = ((bf16[128,288,128]{2,1,0:T(8,128)(2,1)}), bf16[128,288,128]{2,1,0:T(8,128)(2,1)}, u32[]{:S(2)}, u32[]{:S(2)}) async-start(bf16[128,288,128]{2,1,0:T(8,128)(2,1)} %reshape.126), calls=%async_computation.3 | async-start | bytes 18874368 | tf_op jit(solution)/shard_map/all_to_all | solution.py:77
Sparse Core Ops, SparseCore 0:
  157.0 34.1 reduce-scatter.1
